TPU v7x, 256 devices: a whole 4x4x8 slice. The times are simulated.
256 devices in a mesh: dp: 128 (over z, x_lo, y, core), tensor: 2 (over x_hi).
Axes of the slice: x: 4 (x_hi: 2, x_lo: 2; x = x_hi * 2 + x_lo), y: 4, z: 8, core: 2. Of those that a mesh axis runs over, the one named last changes fastest.
Arguments:
- looked: bfloat16 [8192, 16384], P(('dp', 'tensor')), may hold values from -6 to 6
- column_owner: int32 [8192], replicated, may hold values from 0 to 8191, each once
- v_proj: bfloat16 [384, 8192], P(None, 'tensor'), may hold values from -0.0625 to 0.0625
- u_proj: bfloat16 [384, 8192], P(None, 'tensor'), may hold values from -0.3125 to 0.3125
- bias: float32 [8192], P('tensor'), may hold values from -3 to 3
- upstream: bfloat16 [8192, 16384], P('tensor', 'dp'), may hold values from -6 to 6
Outputs:
- d_looked: bfloat16 [8192, 16384], P(('dp', 'tensor'))
- grad_u: float32 [384, 8192], P('dp', 'tensor')
- grad_v: float32 [384, 8192], P('dp', 'tensor')
- grad_bias: float32 [8192], P('tensor')
Inputs may be any that keep to these rules, and one draw needn't show every extreme that they name: A permutation of the 8192 feature columns: wire row r carries column column_owner[r].
All inputs are finite; a program needn't handle non-finite values.
Results may differ from a plain program's by a relative error of at most 0.0049.
Values may be sent and summed in bfloat16 or wider, within the bound.
No kernel may reach another device: no remote copies, remote signals or barrier semaphores. Data moves between devices by JAX's collectives and lax.ppermute only.
A program may use at most 128 MiB of HBM per device.

v0:
```python
import math
import jax
import jax.numpy as jnp
from jax import lax
from jax.sharding import PartitionSpec as P


def contract_last(left, right):
    return lax.dot_general(
        left, right, (((1,), (1,)), ((), ())), preferred_element_type=jnp.float32
    )


def contract_first(left, right):
    return lax.dot_general(
        left, right, (((0,), (0,)), ((), ())), preferred_element_type=jnp.float32
    )


def rank_cotangent(u_proj, scaled16):
    dh_part = jnp.dot(u_proj, scaled16, preferred_element_type=jnp.float32)
    return lax.psum(dh_part, "tensor").astype(jnp.bfloat16)


def per_device(looked, column_owner, v_proj, u_proj, bias, upstream):
    dp_count = lax.axis_size("dp")
    pair_count = lax.axis_size("tensor")
    pair_index = lax.axis_index("tensor")
    block_rows = looked.shape[0]
    half_width = v_proj.shape[1]
    full_width = half_width * pair_count
    local_samples = upstream.shape[1]
    norm = 1.0 / math.sqrt(local_samples * dp_count)
    wire_ids = jnp.arange(full_width, dtype=jnp.int32)
    inverse = jnp.zeros((full_width,), jnp.int32).at[column_owner].set(wire_ids)
    mine_wire = lax.dynamic_slice_in_dim(inverse, pair_index * half_width, half_width)
    arrived = lax.all_to_all(looked, "dp", split_axis=1, concat_axis=0, tiled=True)
    paired = lax.all_gather(arrived, "tensor", axis=0, tiled=True)
    block_ids = mine_wire // block_rows
    within = mine_wire % block_rows
    gather_rows = (
        block_ids % pair_count * (dp_count * block_rows)
        + block_ids // pair_count * block_rows
        + within
    )
    x_zero = jnp.take(paired, gather_rows, axis=0)
    h_part = jnp.dot(v_proj, x_zero, preferred_element_type=jnp.float32)
    hrank = lax.psum(h_part, "tensor").astype(jnp.bfloat16)
    mix = contract_first(u_proj, hrank) + bias[:, None]
    cotan = upstream.astype(jnp.float32)
    scaled = cotan * x_zero.astype(jnp.float32)
    scaled16 = scaled.astype(jnp.bfloat16)
    grad_bias = lax.psum(jnp.sum(scaled, axis=1), "dp") * norm
    dhrank = rank_cotangent(u_proj, scaled16)
    first = contract_last(hrank, scaled16)
    second = contract_last(dhrank, x_zero)
    joined_grads = (
        lax.psum_scatter(
            jnp.concatenate([first, second], axis=1), "dp", scatter_dimension=0, tiled=True
        )
        * norm
    )
    grad_u = joined_grads[:, :half_width]
    grad_v = joined_grads[:, half_width:]
    dx_zero = (cotan * (mix + 1.0) + contract_first(v_proj, dhrank)).astype(jnp.bfloat16)
    dx_full = lax.all_gather(dx_zero, "tensor", axis=0, tiled=True)
    send_wire = (
        (jnp.arange(dp_count, dtype=jnp.int32)[:, None] * pair_count + pair_index) * block_rows
        + jnp.arange(block_rows, dtype=jnp.int32)[None, :]
    ).reshape(-1)
    send_cols = jnp.take(column_owner, send_wire, axis=0)
    outgoing = jnp.take(dx_full, send_cols, axis=0)
    d_looked = lax.all_to_all(outgoing, "dp", split_axis=0, concat_axis=1, tiled=True)
    return (d_looked, grad_u, grad_v, grad_bias)


def solution(mesh):
    in_specs = (
        P(("dp", "tensor"), None),
        P(),
        P(None, "tensor"),
        P(None, "tensor"),
        P("tensor"),
        P("tensor", "dp"),
    )
    out_specs = (P(("dp", "tensor"), None), P("dp", "tensor"), P("dp", "tensor"), P("tensor"))
    return jax.shard_map(
        per_device, mesh=mesh, in_specs=in_specs, out_specs=out_specs, check_vma=False
    )
```

profile of v0, /device:TPU:4, one launch (start us, length us, event | category | flops | bytes accessed | tf_op | source)
XLA Modules:
  0.0 1323.6 jit_solution(17877898504607642298)
XLA Ops:
  7.2 0.0 copy-start
  7.2 0.0 all-gather.3.cloned.1.call-start
  7.2 1.6 copy_bitcast_fusion.1
  8.8 0.0 copy-start.1
  8.8 43.1 %all_to_all.38 = bf16[32,128,128]{2,0,1:T(8,128)(2,1)} all-to-all(bf16[32,128,128]{2,0,1:T(8,128)(2,1)S(1)} %copy_bitcast_fusion.1), channel_id=1, replica_groups=mesh['dp'=128,'tensor'=2] {'dp'}, dimensions={1} | all-to-all | bytes 2097152 | tf_op jit(solution)/shard_map/all_to_all | solution.py:37
  51.9 0.0 all-gather.3.cloned.1.call-update
  52.0 0.0 all-gather.5.cloned.1.call-start
  52.0 2.3 copy.20
  54.3 0.0 copy-done.1
  54.3 30.5 %scatter_custom_fusion = s32[8192]{0:T(1024)S(1)} fusion(s32[8192]{0:T(1024)S(1)} %compare_select_fusion.1, s32[8192]{0:T(1024)S(1)} %iota.12, s32[]{:T(128)} %constant.77.clone.1), kind=kCustom, calls=%fused_computation.54 | custom fusion | bytes 32772 | tf_op jit(solution)/shard_map/scatter | solution.py:35
  84.8 0.1 compare_and_fusion.1
  84.9 0.5 all-gather.3.cloned.1.call-done
  85.3 16.1 %gather_fusion.1 = bf16[4096,128]{1,0:T(8,128)(2,1)} fusion(bf16[8192,128]{1,0:T(8,128)(2,1)} %all-gather.3.cloned.1.call-done, s32[4096]{0:T(1024)S(1)} %broadcast_clamp_fusion.1), kind=kCustom, calls=%fused_computation.clone | custom fusion | bytes 2113536 | tf_op jit(solution)/shard_map/jit(_take)/gather | solution.py:46
  101.4 2.3 copy.22
  103.7 0.0 copy-start.3
  103.7 0.0 copy-start.5
  103.7 0.0 copy-done
  103.7 3.4 convolution_bitcast_fusion.1
  107.2 0.0 copy-done.3
  107.2 0.0 copy-done.5
  107.2 0.0 copy-start.7
  107.2 1.7 convolution_bitcast_fusion.2
  108.9 17.8 %all-reduce.6 = (bf16[384,128]{0,1:T(8,128)(2,1)S(1)}, bf16[384,128]{0,1:T(8,128)(2,1)S(1)}) all-reduce(f32[384,128]{0,1:T(8,128)} %convolution_bitcast_fusion.2, f32[384,128]{0,1:T(8,128)} %convolution_bitcast_fusion.1), channel_id=1, replica_groups=mesh['dp'=128,'tensor'=2] {'tensor'}, use_global_device_ids=true, to_apply=%region_1.3 | all-reduce | flops 98304 | bytes 589824 | tf_op jit(solution)/shard_map/psum | solution.py:48
  126.7 0.0 copy-done.7
  126.7 0.0 copy-start.6
  126.8 2.1 fusion.3
  128.9 0.1 copy-done.6
  129.0 1.7 fusion.4
  130.7 0.0 all-gather.5.cloned.1.call-update
  130.7 0.2 all-reduce.5.cloned.1.call-start
  130.9 0.0 copy-start.2
  130.9 0.0 copy-start.4
  131.0 5.0 fusion.7
  135.9 0.0 copy-done.2
  135.9 0.0 copy-done.4
  135.9 3.6 fusion.10
  139.5 10.8 pad_maximum_fusion
  150.3 0.0 all-reduce.5.cloned.1.call-update
  150.4 0.1 iota_add_fusion
  150.4 0.1 add.141
  150.5 0.1 add.144
  150.7 23.0 %gather_fusion = s32[4096]{0:T(1024)S(1)} fusion(s32[8192]{0:T(1024)S(1)} %copy-done.1, s32[4096]{0:T(1024)S(1)} %broadcast_clamp_fusion.2), kind=kCustom, calls=%fused_computation.2 | custom fusion | bytes 49152 | tf_op jit(solution)/shard_map/jit(_take)/gather | solution.py:71
  173.7 0.0 all-gather.5.cloned.1.call-done
  173.8 4.1 copy.23
  177.9 16.1 %gather_fusion.2 = bf16[4096,128]{1,0:T(8,128)(2,1)} fusion(bf16[8192,128]{1,0:T(8,128)(2,1)} %copy.23, s32[4096]{0:T(1024)S(1)} %broadcast_clamp_fusion), kind=kCustom, calls=%fused_computation.1.clone | custom fusion | bytes 2113536 | tf_op jit(solution)/shard_map/jit(_take)/gather | solution.py:72
  193.9 0.0 copy-start.8
  193.9 4.2 broadcast_select_fusion
  198.2 12.8 all-to-all-start.1
  211.0 0.0 copy-done.8
  211.0 0.6 dynamic-slice
  212.3 1.9 fusion.5
  214.2 564.8 %psum.23 = f32[4096]{0:T(1024)S(1)} all-reduce(f32[4096]{0:T(1024)S(1)} %fusion.5), channel_id=1, replica_groups=mesh['dp'=128,'tensor'=2] {'dp'}, use_global_device_ids=true, to_apply=%region_5.7 | all-reduce | flops 4096 | bytes 32768 | tf_op jit(solution)/shard_map/psum | solution.py:53
  779.0 0.6 broadcast_multiply_fusion
  779.7 0.0 all-to-all-done.1
  779.7 2.3 copy_bitcast_fusion
  781.9 533.3 %all-reduce.5.cloned.1.call-done = f32[384,8192]{1,0:T(8,128)} async-done(((f32[384,8192]{1,0:T(8,128)}), f32[384,8192]{1,0:T(8,128)}) %all-reduce.5.cloned.1.call-update) | async-done | bytes 12582928
  1315.3 1.1 dynamic-slice_multiply_fusion
  1316.3 0.7 fusion.33
  (8 shorter events, 0.1 us)
Async XLA Ops:
  7.2 96.6 %copy-start = (bf16[384,4096]{1,0:T(8,128)(2,1)S(1)}, bf16[384,4096]{1,0:T(8,128)(2,1)}, u32[]{:S(2)}) copy-start(bf16[384,4096]{1,0:T(8,128)(2,1)} %param.11) | copy-start | bytes 9437188
  7.2 78.2 %all-gather.3.cloned.1.call-start = ((), (), s32[]{:S(2)}) async-start(), calls=%async_computation.2 | async-start | bytes 3145728 | tf_op jit(solution)/shard_map/all_gather | solution.py:38
  8.8 45.5 %copy-start.1 = (s32[8192]{0:T(1024)S(1)}, s32[8192]{0:T(1024)}, u32[]{:S(2)}) copy-start(s32[8192]{0:T(1024)} %param.9) | copy-start | bytes 98308
  52.0 121.8 %all-gather.5.cloned.1.call-start = ((), (), s32[]{:S(2)}) async-start(), calls=%async_computation.3 | async-start | bytes 3145728 | tf_op jit(solution)/shard_map/all_gather | solution.py:66
  103.7 3.4 copy-start.3
  103.7 3.4 copy-start.5
  107.2 19.6 %copy-start.7 = (f32[4096]{0:T(1024)S(1)}, f32[4096]{0:T(1024)}, u32[]{:S(2)}) copy-start(f32[4096]{0:T(1024)} %param.12) | copy-start | bytes 49156
  126.7 2.2 copy-start.6
  130.7 1184.6 %all-reduce.5.cloned.1.call-start = ((), (), s32[]{:S(2)}) async-start(), calls=%async_computation.4 | async-start | bytes 25165824
  130.9 5.0 copy-start.2
  130.9 5.0 copy-start.4
  193.9 17.1 %copy-start.8 = (u32[256]{0:T(256)S(1)}, u32[256]{0:T(256)}, u32[]{:S(2)}) copy-start(u32[256]{0:T(256)} %constant.95) | copy-start | bytes 3076
  198.2 581.5 %all-to-all-start.1 = ((bf16[128,32,128]{2,1,0:T(8,128)(2,1)}), bf16[128,32,128]{2,1,0:T(8,128)(2,1)}, u32[]{:S(2)}, u32[]{:S(2)}) async-start(bf16[128,32,128]{2,1,0:T(8,128)(2,1)} %bitcast.41), calls=%async_computation.1 | async-start | bytes 2097152 | tf_op jit(solution)/shard_map/all_to_all | solution.py:73
Sparse Core Ops, SparseCore 0:
  52.1 33.2 all-gather.2
  130.8 38.3 all-gather.4
  171.8 1143.4 all-reduce.4
where the time goes:
time: 1320 us
  blocking collectives  626 us (47%)
  waiting for transfers between devices  534 us (40%)
  local copies, waits for them, and re-layouts  99.7 us (8%)
  other arithmetic  18.8 us (1%)
  matrix products  17.6 us (1%)
  between operations  14.6 us (1%)
    psum x1, blocking collectives, per_device(): grad_bias = lax.psum(jnp.sum(scaled, axis=1), 'dp') * norm  565 us
    unnamed x4, waiting for transfers between devices  533 us
    all_to_all x1, blocking collectives, per_device(): lax.all_to_all(looked, 'dp', split_axis=1, concat_axis=0, tiled=True)  43.1 us
    scatter x1, local copies, waits for them, and re-layouts, per_device(): inverse = jnp.zeros((full_width,), jnp.int32).at[column_owner].set(wire_ids)  30.5 us
  transfers between devices with their start and end apart: 4, of which 2 were waited for; matrix products, arithmetic and copies ran while one was open for 8% of the time, Pallas kernels for 0%

commit v1 on v0

--- a/solution.py
+++ b/solution.py
@@ -23,6 +23,10 @@
 
 
 def per_device(looked, column_owner, v_proj, u_proj, bias, upstream):
+
+    def figure_fit(base_x):
+        return jnp.sum(lax.all_gather(base_x, axis_name="dp"), 0)
+
     dp_count = lax.axis_size("dp")
     pair_count = lax.axis_size("tensor")
     pair_index = lax.axis_index("tensor")
@@ -50,7 +54,7 @@
     cotan = upstream.astype(jnp.float32)
     scaled = cotan * x_zero.astype(jnp.float32)
     scaled16 = scaled.astype(jnp.bfloat16)
-    grad_bias = lax.psum(jnp.sum(scaled, axis=1), "dp") * norm
+    grad_bias = figure_fit(jnp.sum(scaled, axis=1)) * norm
     dhrank = rank_cotangent(u_proj, scaled16)
     first = contract_last(hrank, scaled16)
     second = contract_last(dhrank, x_zero)

time: 1320 us -> 1530 us (1.16)
  waiting for transfers between devices: 534 us -> 1310 us
  blocking collectives: 626 us -> 60.9 us
    unnamed x4 -> x5, waiting for transfers between devices: 533 us -> 1130 us
    psum x1 -> x0, blocking collectives: 565 us -> none  [per_device(): grad_bias = lax.psum(jnp.sum(scaled, axis=1), 'dp') * norm]
    all_gather x0 -> x1, waiting for transfers between devices: none -> 184 us  [figure_fit(): return jnp.sum(lax.all_gather(base_x, axis_name='dp'), 0)]
  transfers between devices with their start and end apart: 4 -> 5, of which waited for: 2 -> 3; matrix products, arithmetic and copies ran while one was open for 8% -> 7% of each run, Pallas kernels for 0% -> 0%
where the time goes in v1:
time: 1530 us
  waiting for transfers between devices  1310 us (86%)
  local copies, waits for them, and re-layouts  97.8 us (6%)
  blocking collectives  60.9 us (4%)
  other arithmetic  18.1 us (1%)
  matrix products  16.3 us (1%)
    unnamed x5, waiting for transfers between devices  1130 us
    all_gather x1, waiting for transfers between devices, figure_fit(): return jnp.sum(lax.all_gather(base_x, axis_name='dp'), 0)  184 us
    all_to_all x1, blocking collectives, per_device(): lax.all_to_all(looked, 'dp', split_axis=1, concat_axis=0, tiled=True)  43.1 us
  transfers between devices with their start and end apart: 5, of which 3 were waited for; matrix products, arithmetic and copies ran while one was open for 7% of the time, Pallas kernels for 0%

profile of v1, /device:TPU:4, one launch (start us, length us, event | category | flops | bytes accessed | tf_op | source)
XLA Modules:
  0.0 1532.6 jit_solution(14096320162784187307)
XLA Ops:
  7.2 0.0 copy-start
  7.2 0.0 all-gather.5.cloned.1.call-start
  7.2 1.6 copy_bitcast_fusion.1
  8.8 43.1 %all_to_all.38 = bf16[32,128,128]{2,0,1:T(8,128)(2,1)} all-to-all(bf16[32,128,128]{2,0,1:T(8,128)(2,1)S(1)} %copy_bitcast_fusion.1), channel_id=1, replica_groups=mesh['dp'=128,'tensor'=2] {'dp'}, dimensions={1} | all-to-all | bytes 2097152 | tf_op jit(solution)/shard_map/all_to_all | solution.py:41
  51.9 0.0 copy-start.2
  51.9 0.0 all-gather.5.cloned.1.call-update
  52.0 0.0 all-gather.7.cloned.1.call-start
  52.0 2.3 copy.25
  54.3 0.0 copy-done.2
  54.3 30.5 %scatter_custom_fusion = s32[8192]{0:T(1024)S(1)} fusion(s32[8192]{0:T(1024)S(1)} %compare_select_fusion.1, s32[8192]{0:T(1024)S(1)} %iota.12, s32[]{:T(128)} %constant.77.clone.1), kind=kCustom, calls=%fused_computation.54 | custom fusion | bytes 32772 | tf_op jit(solution)/shard_map/scatter | solution.py:39
  84.8 0.1 compare_and_fusion.1
  84.9 0.5 all-gather.5.cloned.1.call-done
  85.3 16.1 %gather_fusion.1 = bf16[4096,128]{1,0:T(8,128)(2,1)} fusion(bf16[8192,128]{1,0:T(8,128)(2,1)} %all-gather.5.cloned.1.call-done, s32[4096]{0:T(1024)S(1)} %broadcast_clamp_fusion.1), kind=kCustom, calls=%fused_computation.clone | custom fusion | bytes 2113536 | tf_op jit(solution)/shard_map/jit(_take)/gather | solution.py:50
  101.4 2.3 copy.27
  103.7 0.0 copy-done
  103.7 0.0 copy-start.4
  103.7 0.0 copy-start.6
  103.7 3.4 convolution_bitcast_fusion.1
  107.1 0.0 copy-done.4
  107.1 0.0 copy-done.6
  107.1 0.0 copy-start.8
  107.1 1.8 convolution_bitcast_fusion.2
  108.9 17.8 %all-reduce.6 = (bf16[384,128]{0,1:T(8,128)(2,1)S(1)}, bf16[384,128]{0,1:T(8,128)(2,1)S(1)}) all-reduce(f32[384,128]{0,1:T(8,128)} %convolution_bitcast_fusion.2, f32[384,128]{0,1:T(8,128)} %convolution_bitcast_fusion.1), channel_id=1, replica_groups=mesh['dp'=128,'tensor'=2] {'tensor'}, use_global_device_ids=true, to_apply=%region_1.3 | all-reduce | flops 98304 | bytes 589824 | tf_op jit(solution)/shard_map/psum | solution.py:52
  126.7 0.0 copy-done.8
  126.7 0.0 copy-start.7
  126.7 2.1 fusion.3
  128.8 0.1 copy-done.7
  128.9 0.0 copy-start.3
  128.9 0.0 copy-start.5
  128.9 1.8 fusion.4
  130.7 0.0 all-gather.7.cloned.1.call-update
  130.8 0.0 all-gather.9.cloned.1.call-start
  130.8 0.0 copy-done.3
  130.8 0.0 copy-done.5
  130.8 1.0 fusion.5
  131.8 0.0 all-gather.9.cloned.1.call-update
  131.9 0.2 all-reduce.5.cloned.1.call-start
  132.1 3.6 fusion.7
  135.7 3.6 fusion.10
  139.3 10.7 pad_maximum_fusion
  149.9 0.0 all-reduce.5.cloned.1.call-update
  150.0 0.1 iota_add_fusion
  150.1 0.1 add.139
  150.1 0.1 add.142
  150.3 23.0 %gather_fusion = s32[4096]{0:T(1024)S(1)} fusion(s32[8192]{0:T(1024)S(1)} %copy-done.2, s32[4096]{0:T(1024)S(1)} %broadcast_clamp_fusion.2), kind=kCustom, calls=%fused_computation.2 | custom fusion | bytes 49152 | tf_op jit(solution)/shard_map/jit(_take)/gather | solution.py:75
  173.4 0.0 all-gather.7.cloned.1.call-done
  173.4 3.2 copy.28
  176.6 12.1 gather_fusion.2
  188.8 0.0 copy-start.9
  188.8 2.9 broadcast_select_fusion
  191.7 12.8 all-to-all-start.1
  204.5 0.0 copy-done.9
  204.5 0.6 dynamic-slice
  205.8 183.5 %all-gather.9.cloned.1.call-done = f32[524288]{0:T(1024)} async-done(((f32[4096]{0:T(1024)}), f32[524288]{0:T(1024)}) %all-gather.9.cloned.1.call-update) | async-done | bytes 2097168 | tf_op jit(solution)/shard_map/all_gather | solution.py:28
  389.3 0.0 copy-start.1
  389.3 2.9 reshape.100
  392.2 1.7 reduce_sum.19
  393.9 0.6 broadcast_multiply_fusion
  394.5 0.0 all-to-all-done.1
  394.5 2.3 copy_bitcast_fusion
  396.8 1127.5 %all-reduce.5.cloned.1.call-done = f32[384,8192]{1,0:T(8,128)} async-done(((f32[384,8192]{1,0:T(8,128)}), f32[384,8192]{1,0:T(8,128)}) %all-reduce.5.cloned.1.call-update) | async-done | bytes 12582928
  1524.3 1.1 dynamic-slice_multiply_fusion
  1525.3 0.7 fusion.33
  1526.0 0.0 copy-done.1
  (8 shorter events, 0.1 us)
Async XLA Ops:
  7.2 96.5 %copy-start = (bf16[384,4096]{1,0:T(8,128)(2,1)S(1)}, bf16[384,4096]{1,0:T(8,128)(2,1)}, u32[]{:S(2)}) copy-start(bf16[384,4096]{1,0:T(8,128)(2,1)} %param.11) | copy-start | bytes 9437188
  7.2 78.1 %all-gather.5.cloned.1.call-start = ((), (), s32[]{:S(2)}) async-start(), calls=%async_computation.2 | async-start | bytes 3145728 | tf_op jit(solution)/shard_map/all_gather | solution.py:42
  51.9 2.4 copy-start.2
  52.0 121.4 %all-gather.7.cloned.1.call-start = ((), (), s32[]{:S(2)}) async-start(), calls=%async_computation.3 | async-start | bytes 3145728 | tf_op jit(solution)/shard_map/all_gather | solution.py:70
  103.7 3.4 copy-start.4
  103.7 3.4 copy-start.6
  107.1 19.6 %copy-start.8 = (f32[4096]{0:T(1024)S(1)}, f32[4096]{0:T(1024)}, u32[]{:S(2)}) copy-start(f32[4096]{0:T(1024)} %param.12) | copy-start | bytes 49156
  126.7 2.2 copy-start.7
  128.9 1.9 copy-start.3
  128.9 1.9 copy-start.5
  130.8 258.5 %all-gather.9.cloned.1.call-start = ((), (), s32[]{:S(2)}) async-start(), calls=%async_computation.4 | async-start | bytes 2113536 | tf_op jit(solution)/shard_map/all_gather | solution.py:28
  131.9 1392.4 %all-reduce.5.cloned.1.call-start = ((), (), s32[]{:S(2)}) async-start(), calls=%async_computation.5 | async-start | bytes 25165824
  188.8 15.7 %copy-start.9 = (u32[256]{0:T(256)S(1)}, u32[256]{0:T(256)}, u32[]{:S(2)}) copy-start(u32[256]{0:T(256)} %constant.95) | copy-start | bytes 3076
  191.7 202.8 %all-to-all-start.1 = ((bf16[128,32,128]{2,1,0:T(8,128)(2,1)}), bf16[128,32,128]{2,1,0:T(8,128)(2,1)}, u32[]{:S(2)}, u32[]{:S(2)}) async-start(bf16[128,32,128]{2,1,0:T(8,128)(2,1)} %bitcast.7), calls=%async_computation.1 | async-start | bytes 2097152 | tf_op jit(solution)/shard_map/all_to_all | solution.py:77
  389.3 1136.7 %copy-start.1 = (bf16[384,4096]{1,0:T(8,128)(2,1)S(1)}, bf16[384,4096]{1,0:T(8,128)(2,1)}, u32[]{:S(2)}) copy-start(bf16[384,4096]{1,0:T(8,128)(2,1)} %param.11) | copy-start | bytes 9437188
Sparse Core Ops, SparseCore 0:
  52.1 33.2 all-gather.4
  130.9 38.3 all-gather.6
  171.7 217.5 all-gather.8
  391.8 1132.4 all-reduce.4
